TPU v7x, 32 devices: a whole 2x2x4 slice. The times are simulated.
32 devices in a mesh: micro: 4 (over z), grid: 8 (over y, x, core).
Axes of the slice: x: 2, y: 2, z: 4, core: 2. Of those that a mesh axis runs over, the one named last changes fastest.
Arguments:
- orbitals: float32 [2, 32, 64, 16, 256], P(None, 'micro', None, 'grid'), may hold values from -14 to 14
- local_potential: float32 [32, 16, 256], P('micro', 'grid'), may hold values from -1 to 1
- projectors: float32 [2, 32, 16, 256], P(None, None, 'grid'), may hold values from -0.09375 to 0.09375
- strengths: float32 [2, 32], replicated, may hold values from 1 to 12
- material: int32 [32], replicated, may hold values from 0 to 1
- proj_kind: int32 [32], replicated, may hold values from 0 to 1
- point_cell: int32 [32], replicated, may hold values from 0 to 1999
- vector_now: float32 [2000], replicated, may hold values from -3 to 3
- vector_old: float32 [2000], replicated, may hold values from -3 to 3
Outputs:
- orbitals_out: float32 [2, 32, 64, 16, 256], P(None, 'micro', None, 'grid')
- vector_field: float32 [2000], replicated
All inputs are finite; a program needn't handle non-finite values.
Results may differ from a plain program's by a relative error of at most 0.0003.
Values sent between devices are 32-bit elements; how exact they have to be, the bound alone decides.
A program may use at most 128 MiB of HBM per device.

v0:
```python
import functools

import jax
import jax.numpy as jnp
from jax import lax
from jax.experimental import pallas as pl
from jax.experimental.pallas import tpu as pltpu
from jax.sharding import PartitionSpec as P

NZ = 16
STEPS = 2
ORDER = 4

SPACING = 0.64
TIME_STEP = 0.05
COURANT = 0.9
COUPLING = 1.0
HIGHEST = lax.Precision.HIGHEST
F32 = jnp.float32
BF16 = jnp.bfloat16


def split(value):
    high = value.astype(BF16)
    low = (value - high.astype(F32)).astype(BF16)
    return jnp.concatenate([high, low], axis=-1)


def stencil_matrix(cells):
    row = lax.broadcasted_iota(jnp.int32, (cells, cells), 0)
    col = lax.broadcasted_iota(jnp.int32, (cells, cells), 1)
    z = col % NZ
    forward = row == (col - z + (z + 1) % NZ)
    backward = row == (col - z + (z + NZ - 1) % NZ)
    y_next = row == (col + NZ) % cells
    y_last = row == (col + cells - NZ) % cells
    one = lambda m: m.astype(F32)
    beside = one(forward) + one(backward) + one(y_next) + one(y_last)
    both = jnp.concatenate([beside, one(forward) - one(backward)], axis=1)
    return jnp.concatenate([both, both], axis=0).astype(BF16)


def nt_dot(left, right):
    return lax.dot_general(left, right, (((1,), (1,)), ((), ())), preferred_element_type=F32)


def step_kernel(
    rows, norm, last, scal_ref, limit_ref, field_ref, side_ref, weight_ref, stencil_ref, mix_ref,
    out_ref, current_ref,
    term_a, term_b, total_ref, parts_ref, back_ref, fore_ref, diag_ref,
):
    planes, cells = total_ref.shape[0], total_ref.shape[2]
    half = rows // 2
    nproj = mix_ref.shape[0] // 4
    a = scal_ref[0]
    k2 = 1.0 / (2.0 * SPACING**2)

    def setup(x, overlap):
        beta = side_ref[x, :nproj, :]
        high = beta.astype(BF16).astype(F32)
        low = beta - high
        zero = jnp.zeros_like(high)
        back_ref[x] = jnp.concatenate([high, high, low, zero], axis=0).astype(BF16)
        fore = jnp.concatenate([high, low, zero, zero], axis=0).astype(BF16)
        fore_ref[x] = jnp.concatenate([fore, fore], axis=1)
        diag_ref[x] = jnp.broadcast_to(
            side_ref[x, nproj:nproj + 1, :] + (3.0 / SPACING**2 + 0.5 * a * a), (8, cells)
        )
        value = field_ref[x, :rows, :]
        total_ref[x] = value
        pieces = split(value)
        parts_ref[x] = pieces
        return overlap + nt_dot(pieces, fore_ref[x])

    overlap = lax.fori_loop(0, planes, setup, jnp.zeros((rows, 4 * nproj), F32))
    lane = lax.broadcasted_iota(jnp.int32, (rows, 4 * nproj), 1)
    middle = (lane >= nproj) & (lane < 2 * nproj)
    slots = (total_ref, term_a, term_b)
    source = total_ref
    for degree in range(1, ORDER + 1):
        target = term_a if degree % 2 == 1 else term_b
        scale = TIME_STEP / degree
        c = jnp.dot(overlap, mix_ref[...], precision=HIGHEST, preferred_element_type=F32) * weight_ref[0:1, :]
        high = c.astype(BF16).astype(F32)
        coefficients = jnp.where(middle, c - high, high).astype(BF16)
        if degree == 1:
            read = lambda x: field_ref[x, :rows, :]
        else:
            read = functools.partial(lambda ref, x: ref[x], source)

        def body(x, overlap, read=read, target=target, scale=scale, coefficients=coefficients, degree=degree):
            up = lax.rem(x + 1, planes)
            down = lax.rem(x + planes - 1, planes)
            both = jnp.dot(parts_ref[x], stencil_ref[...], preferred_element_type=F32)
            nonlocal_part = jnp.dot(coefficients, back_ref[x], preferred_element_type=F32)
            beside = both[:, :cells] + nonlocal_part + (read(up) + read(down))
            drift = both[:, cells:] * (a * (scale / (2.0 * SPACING)))
            diag = diag_ref[x][0:1, :] * scale
            kinetic = diag * read(x) - beside * (k2 * scale)
            new = jnp.concatenate([kinetic[half:] - drift[:half], -kinetic[:half] - drift[half:]], axis=0)
            summed = total_ref[x] + new
            total_ref[x] = summed
            if degree < ORDER:
                target[x] = new
                pieces = split(new)
            else:
                pieces = split(summed)
            parts_ref[x] = pieces
            if degree < ORDER:
                overlap = overlap + nt_dot(pieces, fore_ref[x])
            return overlap

        overlap = lax.fori_loop(0, planes, body, jnp.zeros((rows, 4 * nproj), F32))
        source = target

    row_id = lax.broadcasted_iota(jnp.int32, (half, 1), 0)
    occupied = jnp.where(row_id < limit_ref[0], 1.0, 0.0).astype(F32)

    def current(x, acc):
        gradient = jnp.dot(parts_ref[x], stencil_ref[:, cells:], preferred_element_type=F32) * (0.5 / SPACING)
        value = total_ref[x]
        real, imag = value[:half], value[half:]
        if last:
            out_ref[x, :half, :] = real * occupied
            out_ref[x, half:, :] = imag * occupied
        else:
            out_ref[x] = value
        return acc + (
            real * gradient[half:] - imag * gradient[:half] + a * (real * real + imag * imag)
        )

    acc = lax.fori_loop(0, planes, current, jnp.zeros((half, cells), F32))
    total = jnp.sum(acc * occupied) * norm
    current_ref[...] = jnp.full(current_ref.shape, total, F32)


def run_step(field, side, weights, stencil, mix, a, limit, rows, norm, last):
    planes, _, cells = field.shape
    vmem = pl.BlockSpec(memory_space=pltpu.VMEM)
    smem = pl.BlockSpec(memory_space=pltpu.SMEM)
    return pl.pallas_call(
        functools.partial(step_kernel, rows, norm, last),
        out_shape=(
            jax.ShapeDtypeStruct((planes, rows, cells), F32),
            jax.ShapeDtypeStruct((8, 128), F32),
        ),
        in_specs=[smem, smem, vmem, vmem, vmem, vmem, vmem],
        out_specs=(vmem, vmem),
        scratch_shapes=[
            pltpu.VMEM((planes, rows, cells), F32),
            pltpu.VMEM((planes, rows, cells), F32),
            pltpu.VMEM((planes, rows, cells), F32),
            pltpu.VMEM((planes, rows, 2 * cells), BF16),
            pltpu.VMEM((planes, mix.shape[0], cells), BF16),
            pltpu.VMEM((planes, mix.shape[0], 2 * cells), BF16),
            pltpu.VMEM((planes, 8, cells), F32),
        ],
        compiler_params=pltpu.CompilerParams(vmem_limit_bytes=40 * 1024 * 1024),
        name="propagate",
    )(a.reshape(1), limit.reshape(1), field, side, weights, stencil, mix)


def local(
    orbitals, local_potential, projectors, strengths, material, proj_kind, point_cell,
    vector_now, vector_old, devices, grid,
):
    _, points, orb, mine, cells = orbitals.shape
    assert grid % points == 0 and orb % (grid // points) == 0
    share = grid // points
    own = orb // share
    rows = 2 * own
    nproj = projectors.shape[1]
    micro_index, grid_index = lax.axis_index("micro"), lax.axis_index("grid")
    first_point = micro_index * points
    me = first_point + grid_index // share
    first_orbital = (grid_index % share) * own
    kinds = lax.dynamic_slice_in_dim(proj_kind, first_point, points)
    pick = lambda array: lax.dynamic_index_in_dim(array, me, 0, keepdims=False)
    repeat = lambda array: jnp.repeat(array, share, axis=0)
    packed = jnp.concatenate(
        [
            orbitals.reshape(2, points, share, own, mine, cells)
            .transpose(1, 2, 4, 0, 3, 5)
            .reshape(grid, mine, rows, cells),
            repeat(jnp.take(projectors, kinds, axis=0, mode="clip").transpose(0, 2, 1, 3)),
            repeat(jnp.broadcast_to(local_potential[:, :, None, :], (points, mine, 8, cells))),
        ],
        axis=2,
    )
    packed = lax.all_to_all(packed, "grid", split_axis=0, concat_axis=0, tiled=True)
    packed = packed.reshape(grid * mine, -1, cells)
    field, side = packed, packed[:, rows:]
    my_weights = strengths[pick(proj_kind)] * (-2.0 * SPACING**2)
    weights = jnp.broadcast_to(
        jnp.concatenate([my_weights] * 3 + [jnp.zeros_like(my_weights)])[None], (8, 4 * nproj)
    )
    i = lax.broadcasted_iota(jnp.int32, (4 * nproj, 4 * nproj), 0)
    j = lax.broadcasted_iota(jnp.int32, (4 * nproj, 4 * nproj), 1)
    mix = ((i < 2 * nproj) & (i % nproj == j % nproj)).astype(F32)
    stencil = stencil_matrix(cells)
    my_material = pick(material)
    my_cell = pick(point_cell)
    limit = jnp.where(my_material == 1, orb, orb // 2) - first_orbital
    macro_ids = jnp.arange(vector_now.shape[0], dtype=jnp.int32)
    placement = (repeat(point_cell)[:, None] == macro_ids[None, :]).astype(F32)
    present, previous = vector_now, vector_old
    for step in range(STEPS):
        a = lax.dynamic_index_in_dim(present, my_cell, 0, keepdims=False)
        field, current = run_step(
            field, side, weights, stencil, mix, a, limit, rows, 2.0 / (orb * grid * mine * cells), step == STEPS - 1
        )
        spread = jnp.broadcast_to(current[None, :1, :], (devices, 1, 128))
        currents = lax.all_to_all(spread, ("micro", "grid"), split_axis=0, concat_axis=0, tiled=True)[:, 0, 0]
        deposit = jnp.dot(currents, placement, precision=HIGHEST)
        extended = jnp.pad(present, 1)
        curvature = extended[2:] + extended[:-2] - 2.0 * present
        following = 2.0 * present - previous + COURANT**2 * curvature - COUPLING * deposit
        previous, present = present, following
    field = lax.all_to_all(
        field.reshape(grid, mine, rows, cells), "grid", split_axis=0, concat_axis=0, tiled=True
    )
    field = field.reshape(points, share, mine, 2, own, cells).transpose(3, 0, 1, 4, 2, 5)
    field = field.reshape(2, points, orb, mine, cells)
    return field, present


def solution(mesh):
    in_specs = (
        P(None, "micro", None, "grid", None),
        P("micro", "grid", None),
        P(None, None, "grid", None),
        P(),
        P(),
        P(),
        P(),
        P(),
        P(),
    )
    out_specs = (P(None, "micro", None, "grid", None), P())
    body = functools.partial(local, devices=mesh.size, grid=mesh.shape["grid"])
    return jax.shard_map(body, mesh=mesh, in_specs=in_specs, out_specs=out_specs, check_vma=False)
```

profile of v0, /device:TPU:0, one launch (start us, length us, event | category | flops | bytes accessed | tf_op | source)
XLA Modules:
  0.0 167.3 jit_solution(17241812136039953110)
XLA Ops:
  0.7 0.9 dynamic_slice.26
  1.6 1.1 gather_fusion
  2.8 0.3 copy.20
  3.0 0.4 copy-done.3
  3.4 1.7 %pad_maximum_fusion = f32[8,2,168,256]{3,2,1,0:T(8,128)} fusion(f32[8,2,8,256]{3,2,1,0:T(8,128)S(1)} %reshape.47, f32[8,2,32,256]{3,2,1,0:T(8,128)S(1)} %copy.21, f32[8,2,128,256]{3,2,1,0:T(8,128)S(1)} %bitcast.32), kind=kLoop, calls=%fused_computation.1 | loop fusion | flops 1376256 | bytes 5505024 | tf_op jit(solution)/shard_map/concatenate | solution.py:180
  5.2 5.3 %all-to-all-start = ((f32[8,2,168,256]{3,2,1,0:T(8,128)}), f32[8,2,168,256]{3,2,1,0:T(8,128)S(1)}, u32[]{:S(2)}, u32[]{:S(2)}) async-start(f32[8,2,168,256]{3,2,1,0:T(8,128)} %pad_maximum_fusion), calls=%async_computation | async-start | bytes 5505024 | tf_op jit(solution)/shard_map/all_to_all | solution.py:190
  10.5 0.6 dynamic_slice.27
  12.4 0.6 dynamic_slice.23
  14.3 0.6 dynamic_slice.25
  16.1 0.6 dynamic_slice.24.scal_ref
  17.9 26.2 %all-to-all-done = f32[8,2,168,256]{3,2,1,0:T(8,128)S(1)} async-done(((f32[8,2,168,256]{3,2,1,0:T(8,128)}), f32[8,2,168,256]{3,2,1,0:T(8,128)S(1)}, u32[]{:S(2)}, u32[]{:S(2)}) %all-to-all-start) | async-done | bytes 2752544 | tf_op jit(solution)/shard_map/all_to_all | solution.py:190
  44.2 33.8 %propagate.2 = (f32[16,128,256]{2,1,0:T(8,128)S(1)}, f32[8,128]{1,0:T(8,128)S(1)}) custom-call(f32[1]{0:T(128)} %dynamic_slice.24.scal_ref, s32[1]{0:T(128)S(6)} %select_n.73.limit_ref, f32[16,168,256]{2,1,0:T(8,128)S(1)} %bitcast.30, f32[16,40,256]{2,1,0:T(8,128)S(1)} %slice.38.side_ref, f32[8,128]{1,0:T(8,128)S(1)} %broadcast_in_dim.34.weight_ref, ...), custom_call_target="tpu_custom_call" | custom-call | tf_op jit(solution)/shard_map/propagate/pallas_call | solution.py:141
  78.1 11.0 %all_to_all.20 = f32[32,1,128]{2,1,0:T(1,128)S(1)} all-to-all(f32[32,1,128]{2,1,0:T(1,128)S(1)} %broadcast_in_dim.36), channel_id=1, replica_groups=mesh['micro'=4,'grid'=8] {'micro','grid'}, dimensions={0} | all-to-all | bytes 32768 | tf_op jit(solution)/shard_map/all_to_all | solution.py:213
  89.0 0.3 slice_reduce_fusion.1
  89.4 0.3 fusion.13
  89.7 0.6 dynamic_slice.29.scal_ref
  90.3 35.0 %propagate.3 = (f32[16,128,256]{2,1,0:T(8,128)}, f32[8,128]{1,0:T(8,128)S(1)}) custom-call(f32[1]{0:T(128)} %dynamic_slice.29.scal_ref, s32[1]{0:T(128)S(6)} %select_n.73.limit_ref, f32[16,128,256]{2,1,0:T(8,128)S(1)} %get-tuple-element.7.field_ref, f32[16,40,256]{2,1,0:T(8,128)S(1)} %slice.38.side_ref, f32[8,128]{1,0:T(8,128)S(1)} %broadcast_in_dim.34.weight_ref, ...), custom_call_target="tpu_custom_call" | custom-call | tf_op jit(solution)/shard_map/propagate/pallas_call | solution.py:141
  125.3 8.9 %all_to_all.21 = f32[32,1,128]{2,1,0:T(1,128)S(1)} all-to-all(f32[32,1,128]{2,1,0:T(1,128)S(1)} %broadcast_in_dim.38), channel_id=1, replica_groups=mesh['micro'=4,'grid'=8] {'micro','grid'}, dimensions={0} | all-to-all | bytes 32768 | tf_op jit(solution)/shard_map/all_to_all | solution.py:213
  134.2 3.6 %all-to-all-start.2 = ((f32[8,2,128,256]{3,2,1,0:T(8,128)}), f32[8,2,128,256]{3,2,1,0:T(8,128)S(1)}, u32[]{:S(2)}, u32[]{:S(2)}) async-start(f32[8,2,128,256]{3,2,1,0:T(8,128)} %bitcast.10), calls=%async_computation.2 | async-start | bytes 4194304 | tf_op jit(solution)/shard_map/all_to_all | solution.py:219
  137.8 0.3 slice_reduce_fusion
  138.1 0.3 fusion.12
  138.4 0.7 add_subtract_fusion
  139.1 25.3 %all-to-all-done.2 = f32[8,2,128,256]{3,2,1,0:T(8,128)S(1)} async-done(((f32[8,2,128,256]{3,2,1,0:T(8,128)}), f32[8,2,128,256]{3,2,1,0:T(8,128)S(1)}, u32[]{:S(2)}, u32[]{:S(2)}) %all-to-all-start.2) | async-done | bytes 2097184 | tf_op jit(solution)/shard_map/all_to_all | solution.py:219
  164.4 3.0 %copy.22 = f32[2,8,64,2,256]{4,3,2,1,0:T(2,128)} copy(f32[2,8,64,2,256]{4,2,0,3,1:T(8,128)S(1)} %bitcast.31) | data formatting | bytes 4194304
  (41 shorter events, 0.7 us)
Async XLA Ops:
  0.6 0.9 copy-start
  0.6 2.1 %copy-start.1 = (f32[2,8,64,2,256]{4,3,2,1,0:T(2,128)S(1)}, f32[2,8,64,2,256]{4,3,2,1,0:T(2,128)}, u32[]{:S(2)}) copy-start(f32[2,8,64,2,256]{4,3,2,1,0:T(2,128)} %param.9) | copy-start | bytes 6291460
  2.7 0.7 copy-start.3
  5.1 5.4 %copy-start.6 = (s32[32]{0:T(128)S(1)}, s32[32]{0:T(128)}, u32[]{:S(2)}) copy-start(s32[32]{0:T(128)} %param.14) | copy-start | bytes 388
  5.1 7.2 %copy-start.8 = (s32[32]{0:T(128)S(1)}, s32[32]{0:T(128)}, u32[]{:S(2)}) copy-start(s32[32]{0:T(128)} %param.15) | copy-start | bytes 388
  5.1 9.1 %copy-start.7 = (s32[32]{0:T(128)S(1)}, s32[32]{0:T(128)}, u32[]{:S(2)}) copy-start(s32[32]{0:T(128)} %param.13) | copy-start | bytes 388
  5.1 11.0 %copy-start.2 = (f32[2000]{0:T(1024)S(1)}, f32[2000]{0:T(1024)}, u32[]{:S(2)}) copy-start(f32[2000]{0:T(1024)} %param.16) | copy-start | bytes 24004
  5.1 12.2 %copy-start.5 = (f32[2,32]{1,0:T(2,128)S(1)}, f32[2,32]{1,0:T(2,128)}, u32[]{:S(2)}) copy-start(f32[2,32]{1,0:T(2,128)} %param.12) | copy-start | bytes 772
  5.2 39.0 %all-to-all-start = ((f32[8,2,168,256]{3,2,1,0:T(8,128)}), f32[8,2,168,256]{3,2,1,0:T(8,128)S(1)}, u32[]{:S(2)}, u32[]{:S(2)}) async-start(f32[8,2,168,256]{3,2,1,0:T(8,128)} %pad_maximum_fusion), calls=%async_computation | async-start | bytes 5505024 | tf_op jit(solution)/shard_map/all_to_all | solution.py:190
  17.8 71.8 %copy-start.4 = (f32[2000]{0:T(1024)S(1)}, f32[2000]{0:T(1024)}, u32[]{:S(2)}) copy-start(f32[2000]{0:T(1024)} %param.17) | copy-start | bytes 24004
  134.2 30.2 %all-to-all-start.2 = ((f32[8,2,128,256]{3,2,1,0:T(8,128)}), f32[8,2,128,256]{3,2,1,0:T(8,128)S(1)}, u32[]{:S(2)}, u32[]{:S(2)}) async-start(f32[8,2,128,256]{3,2,1,0:T(8,128)} %bitcast.10), calls=%async_computation.2 | async-start | bytes 4194304 | tf_op jit(solution)/shard_map/all_to_all | solution.py:219
where the time goes:
time: 168 us; the launch traced here: 167 us
  Pallas kernels  68.8 us (41%)
  waiting for transfers between devices  51.5 us (31%)
  blocking collectives  19.9 us (12%)
  local copies, waits for them, and re-layouts  9.36 us (6%)
  starting transfers between devices  8.95 us (5%)
  between operations  5.38 us (3%)
  other arithmetic  2.95 us (2%)
    pallas_call x2, Pallas kernels, run_step(): pl.pallas_call(functools.partial(step_kernel, rows, norm, last), out_shap...  68.8 us
    all_to_all x1, waiting for transfers between devices, local(): lax.all_to_all(packed, 'grid', split_axis=0, concat_axis=0, tiled=True)  26.2 us
    all_to_all x1, waiting for transfers between devices, local(): lax.all_to_all(field.reshape(grid, mine, rows, cells), 'grid', split_axis...  25.3 us
    all_to_all x2, blocking collectives, local(): lax.all_to_all(spread, ('micro', 'grid'), split_axis=0, concat_axis=0, ti...  19.9 us
    all_to_all x1, starting transfers between devices, local(): lax.all_to_all(packed, 'grid', split_axis=0, concat_axis=0, tiled=True)  5.34 us
    unnamed x20, local copies, waits for them, and re-layouts  3.64 us
    all_to_all x1, starting transfers between devices, local(): lax.all_to_all(field.reshape(grid, mine, rows, cells), 'grid', split_axis...  3.61 us
  transfers between devices with their start and end apart: 2, of which 2 were waited for; matrix products, arithmetic and copies ran while one was open for 2% of the time, Pallas kernels for 0%

commit v1 on v0

v1 whole, which is shorter than its diff:
```python
import functools

import jax
import jax.numpy as jnp
from jax import lax
from jax.experimental import pallas as pl
from jax.experimental.pallas import tpu as pltpu
from jax.sharding import PartitionSpec as P

NZ = 16
STEPS = 2
ORDER = 4
BLOCK = 8
SMALL = 4

SPACING = 0.64
TIME_STEP = 0.05
COURANT = 0.9
COUPLING = 1.0
HIGHEST = lax.Precision.HIGHEST
F32 = jnp.float32
BF16 = jnp.bfloat16


def split(value):
    high = value.astype(BF16)
    low = (value - high.astype(F32)).astype(BF16)
    return jnp.concatenate([high, low], axis=-1)


def stencil_matrix(cells):
    row = lax.broadcasted_iota(jnp.int32, (cells, cells), 0)
    col = lax.broadcasted_iota(jnp.int32, (cells, cells), 1)
    z = col % NZ
    forward = row == (col - z + (z + 1) % NZ)
    backward = row == (col - z + (z + NZ - 1) % NZ)
    y_next = row == (col + NZ) % cells
    y_last = row == (col + cells - NZ) % cells
    one = lambda m: m.astype(F32)
    beside = one(forward) + one(backward) + one(y_next) + one(y_last)
    both = jnp.concatenate([beside, one(forward) - one(backward)], axis=1)
    return jnp.concatenate([both, both], axis=0).astype(BF16)


def nt_dot(left, right):
    return lax.dot_general(left, right, (((1,), (1,)), ((), ())), preferred_element_type=F32)


def macro_update(present, previous, deposit, macro):
    high, lanes = present.shape
    lane = lax.broadcasted_iota(jnp.int32, present.shape, 1)
    flat = lax.broadcasted_iota(jnp.int32, present.shape, 0) * lanes + lane
    ahead = pltpu.roll(present, lanes - 1, 1)
    ahead = jnp.where(lane == lanes - 1, pltpu.roll(ahead, high - 1, 0), ahead)
    behind = pltpu.roll(present, 1, 1)
    behind = jnp.where(lane == 0, pltpu.roll(behind, 1, 0), behind)
    curvature = ahead + behind - 2.0 * present
    following = 2.0 * present - previous + COURANT**2 * curvature - COUPLING * deposit
    return jnp.where(flat < macro, following, 0.0)


def kernel(
    rows, norm, macro, grid, devices,
    limit_ref, my_cell_ref, cell_ref, field_ref, weight_ref, stencil_ref, mix_ref, now_ref, old_ref,
    out_ref, vector_ref,
    term_a, term_b, total_ref, parts_ref, back_ref, fore_ref, previous_ref,
    mine_ref, currents_ref, send_sem, recv_sem,
):
    planes, cells = total_ref.shape[0], total_ref.shape[2]
    half = rows // 2
    nproj = mix_ref.shape[0] // 4
    k2 = 1.0 / (2.0 * SPACING**2)
    me = lax.axis_index("micro") * grid + lax.axis_index("grid")
    barrier = pltpu.get_barrier_semaphore()

    def peer(distance):
        other = lax.rem(me + distance, devices)
        return other, (other // grid, lax.rem(other, grid))

    @pl.loop(1, devices)
    def _(distance):
        pl.semaphore_signal(barrier, inc=1, device_id=peer(distance)[1], device_id_type=pl.DeviceIdType.MESH)

    def setup(x, overlap):
        beta = field_ref[x, rows:rows + nproj, :]
        high = beta.astype(BF16).astype(F32)
        low = beta - high
        zero = jnp.zeros_like(high)
        back_ref[x] = jnp.concatenate([high, high, low, zero], axis=0).astype(BF16)
        fore = jnp.concatenate([high, low, zero, zero], axis=0).astype(BF16)
        fore_ref[x] = jnp.concatenate([fore, fore], axis=1)
        value = field_ref[x, :rows, :]
        total_ref[x] = value
        term_b[x] = value
        pieces = split(value)
        parts_ref[x] = pieces
        return overlap + nt_dot(pieces, fore_ref[x])

    none = jnp.zeros((rows, 4 * nproj), F32)
    overlap = lax.fori_loop(0, planes, setup, none, unroll=SMALL)
    lane = lax.broadcasted_iota(jnp.int32, (rows, 4 * nproj), 1)
    middle = (lane >= nproj) & (lane < 2 * nproj)
    row_id = lax.broadcasted_iota(jnp.int32, (half, 1), 0)
    occupied = jnp.where(row_id < limit_ref[0], 1.0, 0.0).astype(F32)
    flat = (
        lax.broadcasted_iota(jnp.int32, now_ref.shape, 0) * now_ref.shape[1]
        + lax.broadcasted_iota(jnp.int32, now_ref.shape, 1)
    )
    vector_ref[...] = now_ref[...]
    previous_ref[...] = old_ref[...]
    pl.semaphore_wait(barrier, devices - 1)

    def advance(step, overlap):
        a = jnp.sum(jnp.where(flat == my_cell_ref[0], vector_ref[...], 0.0))
        source = term_b
        for degree in range(1, ORDER + 1):
            target = term_a if degree % 2 == 1 else term_b
            scale = TIME_STEP / degree
            c = jnp.dot(overlap, mix_ref[...], precision=HIGHEST, preferred_element_type=F32) * weight_ref[0:1, :]
            high = c.astype(BF16).astype(F32)
            coefficients = jnp.where(middle, c - high, high).astype(BF16)
            base = 3.0 / SPACING**2 + 0.5 * a * a

            def body(block, overlap, source=source, target=target, scale=scale, coefficients=coefficients, degree=degree):
                x0 = block * BLOCK
                pieces = parts_ref[pl.ds(x0, BLOCK)].reshape(BLOCK * rows, 2 * cells)
                stencils = jnp.dot(pieces, stencil_ref[...], preferred_element_type=F32)
                for offset in range(BLOCK):
                    x = x0 + offset
                    up = lax.rem(x + 1, planes)
                    down = lax.rem(x + planes - 1, planes)
                    both = stencils[offset * rows:(offset + 1) * rows]
                    nonlocal_part = jnp.dot(coefficients, back_ref[x], preferred_element_type=F32)
                    beside = both[:, :cells] + nonlocal_part + (source[up] + source[down])
                    drift = both[:, cells:] * (a * (scale / (2.0 * SPACING)))
                    diag = (field_ref[x, rows + nproj:rows + nproj + 1, :] + base) * scale
                    kinetic = diag * source[x] - beside * (k2 * scale)
                    new = jnp.concatenate([kinetic[half:] - drift[:half], -kinetic[:half] - drift[half:]], axis=0)
                    summed = total_ref[x] + new
                    total_ref[x] = summed
                    term = new if degree < ORDER else summed
                    target[x] = term
                    pieces = split(term)
                    parts_ref[x] = pieces
                    overlap = overlap + nt_dot(pieces, fore_ref[x])
                return overlap

            overlap = lax.fori_loop(0, planes // BLOCK, body, none)
            source = target

        def current(x, acc):
            gradient = jnp.dot(parts_ref[x], stencil_ref[:, cells:], preferred_element_type=F32) * (0.5 / SPACING)
            value = total_ref[x]
            real, imag = value[:half], value[half:]
            return acc + (
                real * gradient[half:] - imag * gradient[:half] + a * (real * real + imag * imag)
            )

        acc = lax.fori_loop(0, planes, current, jnp.zeros((half, cells), F32), unroll=SMALL)
        mine_ref[step] = jnp.full((1, 128), jnp.sum(acc * occupied) * norm, F32)

        def copy(distance):
            other, device = peer(distance)
            return pltpu.make_async_remote_copy(
                src_ref=mine_ref.at[step],
                dst_ref=currents_ref.at[step, me],
                send_sem=send_sem.at[step, distance],
                recv_sem=recv_sem.at[step, me],
                device_id=device,
                device_id_type=pl.DeviceIdType.MESH,
            )

        @pl.loop(1, devices)
        def _(distance):
            copy(distance).start()

        currents_ref[step, me] = mine_ref[step]

        @pl.loop(1, devices)
        def _(distance):
            copy(distance).wait_send()
            other = peer(distance)[0]
            pltpu.make_async_remote_copy(
                src_ref=mine_ref.at[step],
                dst_ref=currents_ref.at[step, other],
                send_sem=send_sem.at[step, distance],
                recv_sem=recv_sem.at[step, other],
                device_id=peer(distance)[1],
                device_id_type=pl.DeviceIdType.MESH,
            ).wait_recv()

        def add(source, deposit):
            return deposit + jnp.where(flat == cell_ref[source], currents_ref[step, source], 0.0)

        deposit = lax.fori_loop(0, devices, add, jnp.zeros(flat.shape, F32), unroll=SMALL)
        present = vector_ref[...]
        vector_ref[...] = macro_update(present, previous_ref[...], deposit, macro)
        previous_ref[...] = present
        return overlap

    lax.fori_loop(0, STEPS, advance, overlap)

    def finish(x, carry):
        value = total_ref[x]
        out_ref[x, :half, :] = value[:half] * occupied
        out_ref[x, half:, :] = value[half:] * occupied
        return carry

    lax.fori_loop(0, planes, finish, 0, unroll=SMALL)


def propagate(limit, my_cell, owners, field, weights, stencil, mix, now, old, rows, norm, macro, grid, devices):
    planes, _, cells = field.shape
    vmem = pl.BlockSpec(memory_space=pltpu.VMEM)
    smem = pl.BlockSpec(memory_space=pltpu.SMEM)
    return pl.pallas_call(
        functools.partial(kernel, rows, norm, macro, grid, devices),
        out_shape=(
            jax.ShapeDtypeStruct((planes, rows, cells), F32),
            jax.ShapeDtypeStruct(now.shape, F32),
        ),
        in_specs=[smem] * 3 + [vmem] * 6,
        out_specs=(vmem, vmem),
        scratch_shapes=[
            pltpu.VMEM((planes, rows, cells), F32),
            pltpu.VMEM((planes, rows, cells), F32),
            pltpu.VMEM((planes, rows, cells), F32),
            pltpu.VMEM((planes, rows, 2 * cells), BF16),
            pltpu.VMEM((planes, mix.shape[0], cells), BF16),
            pltpu.VMEM((planes, mix.shape[0], 2 * cells), BF16),
            pltpu.VMEM(now.shape, F32),
            pltpu.VMEM((STEPS, 1, 128), F32),
            pltpu.VMEM((STEPS, devices, 1, 128), F32),
            pltpu.SemaphoreType.DMA((STEPS, devices)),
            pltpu.SemaphoreType.DMA((STEPS, devices)),
        ],
        compiler_params=pltpu.CompilerParams(
            vmem_limit_bytes=40 * 1024 * 1024, collective_id=0, has_side_effects=True
        ),
        name="propagate",
    )(limit.reshape(1), my_cell.reshape(1), owners, field, weights, stencil, mix, now, old)


def local(
    orbitals, local_potential, projectors, strengths, material, proj_kind, point_cell,
    vector_now, vector_old, devices, grid,
):
    _, points, orb, mine, cells = orbitals.shape
    assert grid % points == 0 and orb % (grid // points) == 0
    share = grid // points
    own = orb // share
    rows = 2 * own
    nproj = projectors.shape[1]
    micro_index, grid_index = lax.axis_index("micro"), lax.axis_index("grid")
    first_point = micro_index * points
    me = first_point + grid_index // share
    first_orbital = (grid_index % share) * own
    kinds = lax.dynamic_slice_in_dim(proj_kind, first_point, points)
    pick = lambda array: lax.dynamic_index_in_dim(array, me, 0, keepdims=False)
    repeat = lambda array: jnp.repeat(array, share, axis=0)
    packed = jnp.concatenate(
        [
            orbitals.reshape(2, points, share, own, mine, cells)
            .transpose(1, 2, 4, 0, 3, 5)
            .reshape(grid, mine, rows, cells),
            repeat(jnp.take(projectors, kinds, axis=0, mode="clip").transpose(0, 2, 1, 3)),
            repeat(jnp.broadcast_to(local_potential[:, :, None, :], (points, mine, 8, cells))),
        ],
        axis=2,
    )
    packed = lax.all_to_all(packed, "grid", split_axis=0, concat_axis=0, tiled=True)
    packed = packed.reshape(grid * mine, -1, cells)
    my_weights = strengths[pick(proj_kind)] * (-2.0 * SPACING**2)
    weights = jnp.broadcast_to(
        jnp.concatenate([my_weights] * 3 + [jnp.zeros_like(my_weights)])[None], (8, 4 * nproj)
    )
    i = lax.broadcasted_iota(jnp.int32, (4 * nproj, 4 * nproj), 0)
    j = lax.broadcasted_iota(jnp.int32, (4 * nproj, 4 * nproj), 1)
    mix = ((i < 2 * nproj) & (i % nproj == j % nproj)).astype(F32)
    stencil = stencil_matrix(cells)
    my_material = pick(material)
    my_cell = pick(point_cell)
    limit = jnp.where(my_material == 1, orb, orb // 2) - first_orbital
    macro = vector_now.shape[0]
    wide = (macro // 1024 + 1) * 1024
    lay = lambda vector: jnp.pad(vector, (0, wide - macro)).reshape(-1, 128)
    field, vector = propagate(
        limit, my_cell, repeat(point_cell), packed, weights, stencil, mix, lay(vector_now), lay(vector_old),
        rows, 2.0 / (orb * grid * mine * cells), macro, grid, devices,
    )
    field = lax.all_to_all(
        field.reshape(grid, mine, rows, cells), "grid", split_axis=0, concat_axis=0, tiled=True
    )
    field = field.reshape(points, share, mine, 2, own, cells).transpose(3, 0, 1, 4, 2, 5)
    field = field.reshape(2, points, orb, mine, cells)
    return field, vector.reshape(-1)[:macro]


def solution(mesh):
    in_specs = (
        P(None, "micro", None, "grid", None),
        P("micro", "grid", None),
        P(None, None, "grid", None),
        P(),
        P(),
        P(),
        P(),
        P(),
        P(),
    )
    out_specs = (P(None, "micro", None, "grid", None), P())
    body = functools.partial(local, devices=mesh.size, grid=mesh.shape["grid"])
    return jax.shard_map(body, mesh=mesh, in_specs=in_specs, out_specs=out_specs, check_vma=False)
```

time: 168 us -> 131 us (0.78)
  blocking collectives: 19.9 us -> 0 us
  Pallas kernels: 68.8 us -> 49.6 us
  waiting for transfers between devices: 51.5 us -> 55.1 us
  between operations: 5.38 us -> 3.56 us
    all_to_all x2 -> x0, blocking collectives: 19.9 us -> none  [local(): lax.all_to_all(spread, ('micro', 'grid'), split_axis=0, concat_axis=0, ti...]
    pallas_call x2 -> x1, Pallas kernels: 68.8 us -> 49.6 us  [propagate(): pl.pallas_call(functools.partial(kernel, rows, norm, macro, grid, devices...]
    unnamed x20 -> x21, local copies, waits for them, and re-layouts: 3.64 us -> 6.9 us
    all_to_all x1, waiting for transfers between devices: 26.2 us -> 28.5 us  [local(): lax.all_to_all(packed, 'grid', split_axis=0, concat_axis=0, tiled=True)]
where the time goes in v1:
time: 131 us; the launch traced here: 130 us
  waiting for transfers between devices  55.1 us (42%)
  Pallas kernels  49.6 us (38%)
  local copies, waits for them, and re-layouts  10.7 us (8%)
  starting transfers between devices  9.06 us (7%)
  between operations  3.56 us (3%)
  other arithmetic  2.21 us (2%)
    pallas_call x1, Pallas kernels, propagate(): pl.pallas_call(functools.partial(kernel, rows, norm, macro, grid, devices...  49.6 us
    all_to_all x1, waiting for transfers between devices, local(): lax.all_to_all(packed, 'grid', split_axis=0, concat_axis=0, tiled=True)  28.5 us
    all_to_all x1, waiting for transfers between devices, local(): lax.all_to_all(field.reshape(grid, mine, rows, cells), 'grid', split_axis...  26.6 us
    unnamed x21, local copies, waits for them, and re-layouts  6.9 us
    all_to_all x1, starting transfers between devices, local(): lax.all_to_all(packed, 'grid', split_axis=0, concat_axis=0, tiled=True)  5.34 us
    all_to_all x1, starting transfers between devices, local(): lax.all_to_all(field.reshape(grid, mine, rows, cells), 'grid', split_axis...  3.71 us
  transfers between devices with their start and end apart: 2, of which 2 were waited for; matrix products, arithmetic and copies ran while one was open for 2% of the time, Pallas kernels for 0%

profile of v1, /device:TPU:0, one launch (start us, length us, event | category | flops | bytes accessed | tf_op | source)
XLA Modules:
  0.0 130.2 jit_solution(7109618457065387819)
XLA Ops:
  0.6 0.0 copy-start
  0.7 0.8 dynamic_slice.18
  1.4 0.1 copy-done
  1.6 1.1 gather_fusion
  2.7 0.0 copy-start.3
  2.7 0.1 copy.15
  2.7 1.9 %copy.14 = f32[2,8,64,2,256]{4,2,0,3,1:T(8,128)S(1)} copy(f32[2,8,64,2,256]{4,3,2,1,0:T(2,128)} %param.9) | data formatting | bytes 4194304 | tf_op args[0]
  4.6 1.7 %pad_maximum_fusion = f32[8,2,168,256]{3,2,1,0:T(8,128)} fusion(f32[8,2,8,256]{3,2,1,0:T(8,128)S(1)} %reshape.47, f32[8,2,32,256]{3,2,1,0:T(8,128)S(1)} %copy.15, f32[8,2,128,256]{3,2,1,0:T(8,128)S(1)} %bitcast.26), kind=kLoop, calls=%fused_computation.1 | loop fusion | flops 1376256 | bytes 5505024 | tf_op jit(solution)/shard_map/concatenate | solution.py:261
  6.4 0.0 copy-start.4
  6.4 5.3 %all-to-all-start = ((f32[8,2,168,256]{3,2,1,0:T(8,128)}), f32[8,2,168,256]{3,2,1,0:T(8,128)S(1)}, u32[]{:S(2)}, u32[]{:S(2)}) async-start(f32[8,2,168,256]{3,2,1,0:T(8,128)} %pad_maximum_fusion), calls=%async_computation | async-start | bytes 5505024 | tf_op jit(solution)/shard_map/all_to_all | solution.py:271
  11.8 0.7 dynamic_slice.19
  12.4 0.6 dynamic_slice.16
  13.0 0.6 dynamic_slice.17.my_cell_ref
  16.4 0.1 pad_maximum_fusion.2
  16.5 0.2 fusion.7
  16.8 0.1 fusion.13.mix_ref
  16.9 28.5 %all-to-all-done = f32[8,2,168,256]{3,2,1,0:T(8,128)S(1)} async-done(((f32[8,2,168,256]{3,2,1,0:T(8,128)}), f32[8,2,168,256]{3,2,1,0:T(8,128)S(1)}, u32[]{:S(2)}, u32[]{:S(2)}) %all-to-all-start) | async-done | bytes 2752544 | tf_op jit(solution)/shard_map/all_to_all | solution.py:271
  45.4 49.6 %propagate.1 = (f32[16,128,256]{2,1,0:T(8,128)S(1)}, f32[16,128]{1,0:T(8,128)S(1)}) custom-call(s32[1]{0:T(128)S(6)} %select_n.63.limit_ref, s32[1]{0:T(128)} %dynamic_slice.17.my_cell_ref, s32[32]{0:T(128)S(1)} %copy-done.2, f32[16,168,256]{2,1,0:T(8,128)S(1)} %bitcast.22, f32[8,128]{1,0:T(8,128)S(1)} %broadcast_in_dim.16.weight_ref, ...), custom_call_target="tpu_custom_call" | custom-call | tf_op jit(solution)/shard_map/propagate/pallas_call | solution.py:216
  95.0 0.0 copy-start.1
  95.0 1.3 %copy-done.1 = f32[16,128,256]{2,1,0:T(8,128)} copy-done((f32[16,128,256]{2,1,0:T(8,128)}, f32[16,128,256]{2,1,0:T(8,128)S(1)}, u32[]{:S(2)}) %copy-start.1) | copy-done | bytes 2097176
  96.3 3.7 %all-to-all-start.1 = ((f32[8,2,128,256]{3,2,1,0:T(8,128)}), f32[8,2,128,256]{3,2,1,0:T(8,128)S(1)}, u32[]{:S(2)}, u32[]{:S(2)}) async-start(f32[8,2,128,256]{3,2,1,0:T(8,128)} %bitcast.23), calls=%async_computation.1 | async-start | bytes 4194304 | tf_op jit(solution)/shard_map/all_to_all | solution.py:291
  100.0 26.6 %all-to-all-done.1 = f32[8,2,128,256]{3,2,1,0:T(8,128)S(1)} async-done(((f32[8,2,128,256]{3,2,1,0:T(8,128)}), f32[8,2,128,256]{3,2,1,0:T(8,128)S(1)}, u32[]{:S(2)}, u32[]{:S(2)}) %all-to-all-start.1) | async-done | bytes 2097184 | tf_op jit(solution)/shard_map/all_to_all | solution.py:291
  126.6 2.9 %copy.16 = f32[2,8,64,2,256]{4,3,2,1,0:T(2,128)} copy(f32[2,8,64,2,256]{4,2,0,3,1:T(8,128)S(1)} %bitcast.25) | data formatting | bytes 4194304
  129.6 0.6 copy.18
  (27 shorter events, 0.2 us)
Async XLA Ops:
  0.6 0.9 copy-start
  2.7 2.0 %copy-start.3 = (f32[8,2,256]{2,1,0:T(2,128)S(1)}, f32[8,2,256]{2,1,0:T(2,128)}, u32[]{:S(2)}) copy-start(f32[8,2,256]{2,1,0:T(2,128)} %param.10) | copy-start | bytes 49156
  6.4 5.4 %copy-start.7 = (s32[32]{0:T(128)S(1)}, s32[32]{0:T(128)}, u32[]{:S(2)}) copy-start(s32[32]{0:T(128)} %param.14) | copy-start | bytes 388
  6.4 6.1 %copy-start.8 = (s32[32]{0:T(128)S(1)}, s32[32]{0:T(128)}, u32[]{:S(2)}) copy-start(s32[32]{0:T(128)} %param.13) | copy-start | bytes 388
  6.4 6.6 %copy-start.2 = (s32[32]{0:T(128)S(1)}, s32[32]{0:T(128)}, u32[]{:S(2)}) copy-start(s32[32]{0:T(128)} %cell_ref.1) | copy-start | bytes 388
  6.4 9.9 %copy-start.6 = (f32[2,32]{1,0:T(2,128)S(1)}, f32[2,32]{1,0:T(2,128)}, u32[]{:S(2)}) copy-start(f32[2,32]{1,0:T(2,128)} %param.12) | copy-start | bytes 772
  6.4 10.1 %copy-start.4 = (f32[2000]{0:T(1024)S(1)}, f32[2000]{0:T(1024)}, u32[]{:S(2)}) copy-start(f32[2000]{0:T(1024)} %param.17) | copy-start | bytes 24004
  6.4 10.1 %copy-start.5 = (f32[2000]{0:T(1024)S(1)}, f32[2000]{0:T(1024)}, u32[]{:S(2)}) copy-start(f32[2000]{0:T(1024)} %param.16) | copy-start | bytes 24004
  6.4 39.0 %all-to-all-start = ((f32[8,2,168,256]{3,2,1,0:T(8,128)}), f32[8,2,168,256]{3,2,1,0:T(8,128)S(1)}, u32[]{:S(2)}, u32[]{:S(2)}) async-start(f32[8,2,168,256]{3,2,1,0:T(8,128)} %pad_maximum_fusion), calls=%async_computation | async-start | bytes 5505024 | tf_op jit(solution)/shard_map/all_to_all | solution.py:271
  95.0 1.3 %copy-start.1 = (f32[16,128,256]{2,1,0:T(8,128)}, f32[16,128,256]{2,1,0:T(8,128)S(1)}, u32[]{:S(2)}) copy-start(f32[16,128,256]{2,1,0:T(8,128)S(1)} %get-tuple-element.4) | copy-start | bytes 6291460
  96.3 30.3 %all-to-all-start.1 = ((f32[8,2,128,256]{3,2,1,0:T(8,128)}), f32[8,2,128,256]{3,2,1,0:T(8,128)S(1)}, u32[]{:S(2)}, u32[]{:S(2)}) async-start(f32[8,2,128,256]{3,2,1,0:T(8,128)} %bitcast.23), calls=%async_computation.1 | async-start | bytes 4194304 | tf_op jit(solution)/shard_map/all_to_all | solution.py:291

commit v2 on v1

v2 whole, which is shorter than its diff:
```python
import functools

import jax
import jax.numpy as jnp
from jax import lax
from jax.experimental import pallas as pl
from jax.experimental.pallas import tpu as pltpu
from jax.sharding import PartitionSpec as P

NZ = 16
STEPS = 2
ORDER = 4
BLOCK = 8
SMALL = 4
GROUPS = 1

SPACING = 0.64
TIME_STEP = 0.05
COURANT = 0.9
COUPLING = 1.0
HIGHEST = lax.Precision.HIGHEST
F32 = jnp.float32
BF16 = jnp.bfloat16


def split(value):
    high = value.astype(BF16)
    low = (value - high.astype(F32)).astype(BF16)
    return jnp.concatenate([high, low], axis=-1)


def stencil_matrix(cells):
    row = lax.broadcasted_iota(jnp.int32, (cells, cells), 0)
    col = lax.broadcasted_iota(jnp.int32, (cells, cells), 1)
    z = col % NZ
    forward = row == (col - z + (z + 1) % NZ)
    backward = row == (col - z + (z + NZ - 1) % NZ)
    y_next = row == (col + NZ) % cells
    y_last = row == (col + cells - NZ) % cells
    one = lambda m: m.astype(F32)
    beside = one(forward) + one(backward) + one(y_next) + one(y_last)
    both = jnp.concatenate([beside, one(forward) - one(backward)], axis=1)
    return jnp.concatenate([both, both], axis=0).astype(BF16)


def nt_dot(left, right):
    return lax.dot_general(left, right, (((1,), (1,)), ((), ())), preferred_element_type=F32)


def macro_update(present, previous, deposit, macro):
    high, lanes = present.shape
    lane = lax.broadcasted_iota(jnp.int32, present.shape, 1)
    flat = lax.broadcasted_iota(jnp.int32, present.shape, 0) * lanes + lane
    ahead = pltpu.roll(present, lanes - 1, 1)
    ahead = jnp.where(lane == lanes - 1, pltpu.roll(ahead, high - 1, 0), ahead)
    behind = pltpu.roll(present, 1, 1)
    behind = jnp.where(lane == 0, pltpu.roll(behind, 1, 0), behind)
    curvature = ahead + behind - 2.0 * present
    following = 2.0 * present - previous + COURANT**2 * curvature - COUPLING * deposit
    return jnp.where(flat < macro, following, 0.0)


def kernel(
    norm, macro, grid, devices,
    limit_ref, my_cell_ref, cell_ref, packed_ref, packed_side_ref, weight_ref, stencil_ref, mix_ref, now_ref, old_ref,
    out_ref, vector_ref,
    total_ref, side_ref, term_a, term_b, parts_ref, back_ref, fore_ref, overlap_ref, previous_ref,
    mine_ref, currents_ref, send_sem, recv_sem,
    in_send, in_recv, side_send, side_recv, out_send, out_recv, own_sem,
):
    groups, planes, rows, cells = total_ref.shape
    mine = planes // grid
    half = rows // 2
    nproj = mix_ref.shape[0] // 4
    k2 = 1.0 / (2.0 * SPACING**2)
    here = lax.axis_index("grid")
    layer = lax.axis_index("micro")
    me = layer * grid + here
    barrier = pltpu.get_barrier_semaphore()

    def peer(distance):
        other = lax.rem(me + distance, devices)
        return other, (other // grid, lax.rem(other, grid))

    def beside_me(distance):
        return lax.rem(here + distance, grid)

    def remote(source, target, sent, received, device):
        return pltpu.make_async_remote_copy(
            src_ref=source, dst_ref=target, send_sem=sent, recv_sem=received,
            device_id=device, device_id_type=pl.DeviceIdType.MESH,
        )

    def planes_of(owner):
        return pl.ds(owner * mine, mine)

    def side_copy(distance, owner):
        other = beside_me(distance)
        return remote(
            packed_side_ref.at[other], side_ref.at[planes_of(owner)],
            side_send.at[distance], side_recv.at[owner], (layer, other),
        )

    def in_copy(group, distance, owner):
        other = beside_me(distance)
        return remote(
            packed_ref.at[group, other], total_ref.at[group, planes_of(owner)],
            in_send.at[group, distance], in_recv.at[group, owner], (layer, other),
        )

    def out_copy(group, distance, owner):
        other = beside_me(distance)
        return remote(
            total_ref.at[group, planes_of(other)], out_ref.at[group, owner],
            out_send.at[group, distance], out_recv.at[group, owner], (layer, other),
        )

    def own_side():
        return pltpu.make_async_copy(packed_side_ref.at[here], side_ref.at[planes_of(here)], own_sem.at[0])

    def own_in(group):
        return pltpu.make_async_copy(
            packed_ref.at[group, here], total_ref.at[group, planes_of(here)], own_sem.at[1 + group]
        )

    def own_out(group):
        return pltpu.make_async_copy(
            total_ref.at[group, planes_of(here)], out_ref.at[group, here], own_sem.at[1 + groups + group]
        )

    @pl.loop(1, devices)
    def _(distance):
        pl.semaphore_signal(barrier, inc=1, device_id=peer(distance)[1], device_id_type=pl.DeviceIdType.MESH)

    own_side().start()
    for group in range(groups):
        own_in(group).start()
    vector_ref[...] = now_ref[...]
    previous_ref[...] = old_ref[...]
    pl.semaphore_wait(barrier, devices - 1)

    @pl.loop(1, grid)
    def _(distance):
        side_copy(distance, here).start()

    for group in range(groups):
        @pl.loop(1, grid)
        def _(distance):
            in_copy(group, distance, here).start()

    own_side().wait()

    @pl.loop(1, grid)
    def _(distance):
        side_copy(distance, here).wait_send()
        side_copy(distance, beside_me(distance)).wait_recv()

    def prepare(x, carry):
        beta = side_ref[x, :nproj, :]
        high = beta.astype(BF16).astype(F32)
        low = beta - high
        zero = jnp.zeros_like(high)
        back_ref[x] = jnp.concatenate([high, high, low, zero], axis=0).astype(BF16)
        fore = jnp.concatenate([high, low, zero, zero], axis=0).astype(BF16)
        fore_ref[x] = jnp.concatenate([fore, fore], axis=1)
        return carry

    lax.fori_loop(0, planes, prepare, 0, unroll=SMALL)
    none = jnp.zeros((rows, 4 * nproj), F32)
    lane = lax.broadcasted_iota(jnp.int32, (rows, 4 * nproj), 1)
    middle = (lane >= nproj) & (lane < 2 * nproj)
    row_id = lax.broadcasted_iota(jnp.int32, (half, 1), 0)
    flat = (
        lax.broadcasted_iota(jnp.int32, now_ref.shape, 0) * now_ref.shape[1]
        + lax.broadcasted_iota(jnp.int32, now_ref.shape, 1)
    )

    def advance_group(step, group, a):
        occupied = jnp.where(row_id + group * half < limit_ref[0], 1.0, 0.0).astype(F32)

        @pl.when(step == 0)
        def _():
            own_in(group).wait()

            @pl.loop(1, grid)
            def _(distance):
                in_copy(group, distance, here).wait_send()
                in_copy(group, distance, beside_me(distance)).wait_recv()

            def setup(x, overlap):
                value = total_ref[group, x]
                term_b[group, x] = value
                pieces = split(value)
                parts_ref[group, x] = pieces
                return overlap + nt_dot(pieces, fore_ref[x])

            overlap_ref[group] = lax.fori_loop(0, planes, setup, none, unroll=SMALL)

        overlap = overlap_ref[group]
        source = term_b
        for degree in range(1, ORDER + 1):
            target = term_a if degree % 2 == 1 else term_b
            scale = TIME_STEP / degree
            c = jnp.dot(overlap, mix_ref[...], precision=HIGHEST, preferred_element_type=F32) * weight_ref[0:1, :]
            high = c.astype(BF16).astype(F32)
            coefficients = jnp.where(middle, c - high, high).astype(BF16)
            base = 3.0 / SPACING**2 + 0.5 * a * a

            def body(block, overlap, source=source, target=target, scale=scale, coefficients=coefficients, degree=degree):
                x0 = block * BLOCK
                pieces = parts_ref[group, pl.ds(x0, BLOCK)].reshape(BLOCK * rows, 2 * cells)
                stencils = jnp.dot(pieces, stencil_ref[...], preferred_element_type=F32)
                for offset in range(BLOCK):
                    x = x0 + offset
                    up = lax.rem(x + 1, planes)
                    down = lax.rem(x + planes - 1, planes)
                    both = stencils[offset * rows:(offset + 1) * rows]
                    nonlocal_part = jnp.dot(coefficients, back_ref[x], preferred_element_type=F32)
                    beside = both[:, :cells] + nonlocal_part + (source[group, up] + source[group, down])
                    drift = both[:, cells:] * (a * (scale / (2.0 * SPACING)))
                    diag = (side_ref[x, nproj:nproj + 1, :] + base) * scale
                    kinetic = diag * source[group, x] - beside * (k2 * scale)
                    new = jnp.concatenate([kinetic[half:] - drift[:half], -kinetic[:half] - drift[half:]], axis=0)
                    summed = total_ref[group, x] + new
                    total_ref[group, x] = summed
                    term = new if degree < ORDER else summed
                    target[group, x] = term
                    pieces = split(term)
                    parts_ref[group, x] = pieces
                    overlap = overlap + nt_dot(pieces, fore_ref[x])
                return overlap

            overlap = lax.fori_loop(0, planes // BLOCK, body, none)
            source = target
        overlap_ref[group] = overlap

        @pl.when(step == STEPS - 1)
        def _():
            def mask(x, carry):
                total_ref[group, x, :half, :] = total_ref[group, x, :half, :] * occupied
                total_ref[group, x, half:, :] = total_ref[group, x, half:, :] * occupied
                return carry

            lax.fori_loop(0, planes, mask, 0, unroll=SMALL)

            @pl.loop(1, grid)
            def _(distance):
                out_copy(group, distance, here).start()

            own_out(group).start()

        def current(x, acc):
            gradient = jnp.dot(parts_ref[group, x], stencil_ref[:, cells:], preferred_element_type=F32) * (0.5 / SPACING)
            value = term_b[group, x]
            real, imag = value[:half], value[half:]
            return acc + (
                real * gradient[half:] - imag * gradient[:half] + a * (real * real + imag * imag)
            )

        acc = lax.fori_loop(0, planes, current, jnp.zeros((half, cells), F32), unroll=SMALL)
        return jnp.sum(acc * occupied, axis=0, keepdims=True)

    def copy(step, distance, owner):
        return remote(
            mine_ref.at[step], currents_ref.at[step, owner],
            send_sem.at[step, distance], recv_sem.at[step, owner], peer(distance)[1],
        )

    def advance(step, carry):
        a = jnp.sum(jnp.where(flat == my_cell_ref[0], vector_ref[...], 0.0))
        acc = advance_group(step, 0, a)
        for group in range(1, groups):
            acc = acc + advance_group(step, group, a)
        mine_ref[step] = jnp.full((1, 128), jnp.sum(acc) * norm, F32)

        @pl.loop(1, devices)
        def _(distance):
            copy(step, distance, me).start()

        currents_ref[step, me] = mine_ref[step]

        @pl.loop(1, devices)
        def _(distance):
            copy(step, distance, me).wait_send()
            copy(step, distance, peer(distance)[0]).wait_recv()

        def add(source, deposit):
            return deposit + jnp.where(flat == cell_ref[source], currents_ref[step, source], 0.0)

        deposit = lax.fori_loop(0, devices, add, jnp.zeros(flat.shape, F32), unroll=SMALL)
        present = vector_ref[...]
        vector_ref[...] = macro_update(present, previous_ref[...], deposit, macro)
        previous_ref[...] = present
        return carry

    lax.fori_loop(0, STEPS, advance, 0)
    for group in range(groups):
        own_out(group).wait()

        @pl.loop(1, grid)
        def _(distance):
            out_copy(group, distance, here).wait_send()
            out_copy(group, distance, beside_me(distance)).wait_recv()


def propagate(limit, my_cell, owners, packed, side, weights, stencil, mix, now, old, norm, macro, grid, devices):
    groups, _, mine, rows, cells = packed.shape
    planes = grid * mine
    assert planes % BLOCK == 0
    vmem = pl.BlockSpec(memory_space=pltpu.VMEM)
    smem = pl.BlockSpec(memory_space=pltpu.SMEM)
    anywhere = pl.BlockSpec(memory_space=pl.ANY)
    return pl.pallas_call(
        functools.partial(kernel, norm, macro, grid, devices),
        out_shape=(
            jax.ShapeDtypeStruct(packed.shape, F32),
            jax.ShapeDtypeStruct(now.shape, F32),
        ),
        in_specs=[smem] * 3 + [anywhere] * 2 + [vmem] * 5,
        out_specs=(anywhere, vmem),
        scratch_shapes=[
            pltpu.VMEM((groups, planes, rows, cells), F32),
            pltpu.VMEM((planes,) + side.shape[2:], F32),
            pltpu.VMEM((groups, planes, rows, cells), F32),
            pltpu.VMEM((groups, planes, rows, cells), F32),
            pltpu.VMEM((groups, planes, rows, 2 * cells), BF16),
            pltpu.VMEM((planes, mix.shape[0], cells), BF16),
            pltpu.VMEM((planes, mix.shape[0], 2 * cells), BF16),
            pltpu.VMEM((groups, rows, mix.shape[0]), F32),
            pltpu.VMEM(now.shape, F32),
            pltpu.VMEM((STEPS, 1, 128), F32),
            pltpu.VMEM((STEPS, devices, 1, 128), F32),
            pltpu.SemaphoreType.DMA((STEPS, devices)),
            pltpu.SemaphoreType.DMA((STEPS, devices)),
            pltpu.SemaphoreType.DMA((groups, grid)),
            pltpu.SemaphoreType.DMA((groups, grid)),
            pltpu.SemaphoreType.DMA((grid,)),
            pltpu.SemaphoreType.DMA((grid,)),
            pltpu.SemaphoreType.DMA((groups, grid)),
            pltpu.SemaphoreType.DMA((groups, grid)),
            pltpu.SemaphoreType.DMA((1 + 2 * groups,)),
        ],
        compiler_params=pltpu.CompilerParams(
            vmem_limit_bytes=48 * 1024 * 1024, collective_id=0, has_side_effects=True
        ),
        name="propagate",
    )(limit.reshape(1), my_cell.reshape(1), owners, packed, side, weights, stencil, mix, now, old)


def local(
    orbitals, local_potential, projectors, strengths, material, proj_kind, point_cell,
    vector_now, vector_old, devices, grid,
):
    _, points, orb, mine, cells = orbitals.shape
    assert grid % points == 0 and orb % (grid // points) == 0
    share = grid // points
    own = orb // share
    nproj = projectors.shape[1]
    micro_index, grid_index = lax.axis_index("micro"), lax.axis_index("grid")
    first_point = micro_index * points
    me = first_point + grid_index // share
    first_orbital = (grid_index % share) * own
    kinds = lax.dynamic_slice_in_dim(proj_kind, first_point, points)
    pick = lambda array: lax.dynamic_index_in_dim(array, me, 0, keepdims=False)
    repeat = lambda array: jnp.repeat(array, share, axis=0)
    packed = (
        orbitals.reshape(2, points, share, GROUPS, own // GROUPS, mine, cells)
        .transpose(3, 1, 2, 5, 0, 4, 6)
        .reshape(GROUPS, grid, mine, 2 * own // GROUPS, cells)
    )
    side = repeat(
        jnp.concatenate(
            [
                jnp.take(projectors, kinds, axis=0, mode="clip").transpose(0, 2, 1, 3),
                jnp.broadcast_to(local_potential[:, :, None, :], (points, mine, 8, cells)),
            ],
            axis=2,
        )
    )
    my_weights = strengths[pick(proj_kind)] * (-2.0 * SPACING**2)
    weights = jnp.broadcast_to(
        jnp.concatenate([my_weights] * 3 + [jnp.zeros_like(my_weights)])[None], (8, 4 * nproj)
    )
    i = lax.broadcasted_iota(jnp.int32, (4 * nproj, 4 * nproj), 0)
    j = lax.broadcasted_iota(jnp.int32, (4 * nproj, 4 * nproj), 1)
    mix = ((i < 2 * nproj) & (i % nproj == j % nproj)).astype(F32)
    stencil = stencil_matrix(cells)
    my_material = pick(material)
    my_cell = pick(point_cell)
    limit = jnp.where(my_material == 1, orb, orb // 2) - first_orbital
    macro = vector_now.shape[0]
    wide = (macro // 1024 + 1) * 1024
    lay = lambda vector: jnp.pad(vector, (0, wide - macro)).reshape(-1, 128)
    field, vector = propagate(
        limit, my_cell, repeat(point_cell), packed, side, weights, stencil, mix, lay(vector_now), lay(vector_old),
        2.0 / (orb * grid * mine * cells), macro, grid, devices,
    )
    field = field.reshape(GROUPS, points, share, mine, 2, own // GROUPS, cells).transpose(4, 1, 2, 0, 5, 3, 6)
    field = field.reshape(2, points, orb, mine, cells)
    return field, vector.reshape(-1)[:macro]


def solution(mesh):
    in_specs = (
        P(None, "micro", None, "grid", None),
        P("micro", "grid", None),
        P(None, None, "grid", None),
        P(),
        P(),
        P(),
        P(),
        P(),
        P(),
    )
    out_specs = (P(None, "micro", None, "grid", None), P())
    body = functools.partial(local, devices=mesh.size, grid=mesh.shape["grid"])
    return jax.shard_map(body, mesh=mesh, in_specs=in_specs, out_specs=out_specs, check_vma=False)
```

time: 131 us -> 118 us (0.901)
  waiting for transfers between devices: 55.1 us -> 0 us
  Pallas kernels: 49.6 us -> 101 us
  starting transfers between devices: 9.06 us -> 0 us
    all_to_all x2 -> x0, waiting for transfers between devices: 55.1 us -> none  [the longest x1 28.5 us: local(): lax.all_to_all(packed, 'grid', split_axis=0, concat_axis=0, tiled=True)]
    pallas_call x1, Pallas kernels: 49.6 us -> 101 us  [propagate(): pl.pallas_call(functools.partial(kernel, norm, macro, grid, devices), out...]
    all_to_all x2 -> x0, starting transfers between devices: 9.06 us -> none  [the longest x1 5.34 us: local(): lax.all_to_all(packed, 'grid', split_axis=0, concat_axis=0, tiled=True)]
    unnamed x21 -> x7, local copies, waits for them, and re-layouts: 6.9 us -> 1.27 us
    reshape x1, local copies, waits for them, and re-layouts: 0.01 us -> 2.96 us  [local(): field.reshape(GROUPS, points, share, mine, 2, own // GROUPS, cells)]
    dynamic_slice x3, local copies, waits for them, and re-layouts: 1.83 us -> 3.75 us  [local(): pick = lambda array: lax.dynamic_index_in_dim(array, me, 0, keepdims=False)]
    concatenate x1, other arithmetic: 1.74 us -> 0.06 us  [local(): jnp.concatenate([jnp.take(projectors, kinds, axis=0, mode='clip').transpo...]
  transfers between devices with their start and end apart: 2 -> 0, of which waited for: 2 -> 0; matrix products, arithmetic and copies ran while one was open for 2% -> 0% of each run, Pallas kernels for 0% -> 0%
where the time goes in v2:
time: 118 us
  Pallas kernels  101 us (86%)
  local copies, waits for them, and re-layouts  11.6 us (10%)
  between operations  3.38 us (3%)
  other arithmetic  1.21 us (1%)
    pallas_call x1, Pallas kernels, propagate(): pl.pallas_call(functools.partial(kernel, norm, macro, grid, devices), out...  101 us
    dynamic_slice x3, local copies, waits for them, and re-layouts, local(): pick = lambda array: lax.dynamic_index_in_dim(array, me, 0, keepdims=False)  3.75 us
    reshape x1, local copies, waits for them, and re-layouts, local(): field.reshape(GROUPS, points, share, mine, 2, own // GROUPS, cells)  2.96 us

profile of v2, /device:TPU:0, one launch (start us, length us, event | category | flops | bytes accessed | tf_op | source)
XLA Modules:
  0.0 117.6 jit_solution(7934152598070468524)
XLA Ops:
  0.6 0.0 copy-start
  0.7 1.3 %dynamic_slice.17.my_cell_ref = s32[1]{0:T(128)} dynamic-slice(s32[32]{0:T(128)} %cell_ref.1, s32[]{:T(128)S(6)} %select_n.62), dynamic_slice_sizes={1} | dynamic-slice | bytes 12 | tf_op jit(solution)/shard_map/jit(dynamic_index_in_dim)/dynamic_slice | solution.py:364
  1.9 1.2 %dynamic_slice.19 = s32[1]{0:T(128)} dynamic-slice(s32[32]{0:T(128)} %param.14, s32[]{:T(128)S(6)} %select_n.62), dynamic_slice_sizes={1} | dynamic-slice | bytes 12 | tf_op jit(solution)/shard_map/jit(dynamic_index_in_dim)/dynamic_slice | solution.py:364
  5.1 0.7 dynamic_slice.18
  5.8 1.2 %dynamic_slice.16 = s32[1]{0:T(128)} dynamic-slice(s32[32]{0:T(128)} %param.13, s32[]{:T(128)S(6)} %select_n.62), dynamic_slice_sizes={1} | dynamic-slice | bytes 12 | tf_op jit(solution)/shard_map/jit(dynamic_index_in_dim)/dynamic_slice | solution.py:364
  7.7 0.7 multiply_bitcast_fusion
  8.4 0.1 pad_maximum_fusion.2
  8.6 0.7 pad_bitcast_fusion
  9.3 0.1 fusion.13.mix_ref
  9.5 0.7 broadcast_in_dim.20
  10.2 0.2 fusion.7
  10.4 0.0 copy-start.2
  10.4 0.0 copy-done
  10.4 1.1 gather_fusion
  11.6 0.1 copy.19
  11.6 0.1 pad_maximum_fusion.packed_side_ref
  11.7 0.3 copy-done.2
  12.0 0.0 copy-start.1
  12.0 0.3 copy.13
  12.3 0.4 copy-done.1
  12.6 101.4 %propagate.1 = (f32[1,8,2,128,256]{4,3,2,1,0:T(8,128)S(1)}, f32[16,128]{1,0:T(8,128)S(1)}) custom-call(s32[1]{0:T(128)S(6)} %select_n.63.limit_ref, s32[1]{0:T(128)} %dynamic_slice.17.my_cell_ref, s32[32]{0:T(128)S(1)} %copy-done.1, f32[1,8,2,128,256]{4,3,2,1,0:T(8,128)S(1)} %bitcast.22, f32[8,2,40,256]{3,2,1,0:T(8,128)S(1)} %pad_maximum_fusion.packed_side_ref, ...), custom_call_target="tpu_custom_call" | custom-call | tf_op jit(solution)/shard_map/propagate/pallas_call | solution.py:313
  114.1 3.0 %copy.18 = f32[1,8,1,2,2,64,256]{6,3,5,1,4,0,2:T(2,128)} copy(f32[1,8,1,2,2,64,256]{6,5,4,3,1,2,0:T(8,128)S(1)} %bitcast.23) | data formatting | bytes 4194304 | tf_op jit(solution)/shard_map/reshape | solution.py:398
  117.0 0.6 copy.21
  (12 shorter events, 0.1 us)
Async XLA Ops:
  0.6 9.8 %copy-start = (f32[2,32,2,256]{3,2,1,0:T(2,128)S(1)}, f32[2,32,2,256]{3,2,1,0:T(2,128)}, u32[]{:S(2)}) copy-start(f32[2,32,2,256]{3,2,1,0:T(2,128)} %param.11) | copy-start | bytes 393220
  10.4 1.6 %copy-start.2 = (f32[2,8,64,2,256]{4,3,2,1,0:T(2,128)S(1)}, f32[2,8,64,2,256]{4,3,2,1,0:T(2,128)}, u32[]{:S(2)}) copy-start(f32[2,8,64,2,256]{4,3,2,1,0:T(2,128)} %param.9) | copy-start | bytes 6291460
  12.0 0.7 copy-start.1

commit v3 on v2

--- a/solution.py
+++ b/solution.py
@@ -61,8 +61,8 @@
 
 
 def kernel(
-    norm, macro, grid, devices,
-    limit_ref, my_cell_ref, cell_ref, packed_ref, packed_side_ref, weight_ref, stencil_ref, mix_ref, now_ref, old_ref,
+    norm, macro, share, grid, devices,
+    material_ref, kind_ref, cell_ref, packed_ref, packed_side_ref, weight_ref, stencil_ref, mix_ref, now_ref, old_ref,
     out_ref, vector_ref,
     total_ref, side_ref, term_a, term_b, parts_ref, back_ref, fore_ref, overlap_ref, previous_ref,
     mine_ref, currents_ref, send_sem, recv_sem,
@@ -76,6 +76,13 @@
     here = lax.axis_index("grid")
     layer = lax.axis_index("micro")
     me = layer * grid + here
+    own = groups * half
+    first_orbital = lax.rem(here, share) * own
+    limit = jnp.where(material_ref[me] == 1, share * own, share * own // 2) - first_orbital
+    my_cell, my_kind = cell_ref[me], kind_ref[me]
+    weight = jnp.where(my_kind == 0, weight_ref[0:1, :], 0.0)
+    for kind in range(1, weight_ref.shape[0]):
+        weight = weight + jnp.where(my_kind == kind, weight_ref[kind:kind + 1, :], 0.0)
     barrier = pltpu.get_barrier_semaphore()
 
     def peer(distance):
@@ -176,7 +183,7 @@
     )
 
     def advance_group(step, group, a):
-        occupied = jnp.where(row_id + group * half < limit_ref[0], 1.0, 0.0).astype(F32)
+        occupied = jnp.where(row_id + group * half < limit, 1.0, 0.0).astype(F32)
 
         @pl.when(step == 0)
         def _():
@@ -201,7 +208,7 @@
         for degree in range(1, ORDER + 1):
             target = term_a if degree % 2 == 1 else term_b
             scale = TIME_STEP / degree
-            c = jnp.dot(overlap, mix_ref[...], precision=HIGHEST, preferred_element_type=F32) * weight_ref[0:1, :]
+            c = jnp.dot(overlap, mix_ref[...], precision=HIGHEST, preferred_element_type=F32) * weight
             high = c.astype(BF16).astype(F32)
             coefficients = jnp.where(middle, c - high, high).astype(BF16)
             base = 3.0 / SPACING**2 + 0.5 * a * a
@@ -267,7 +274,7 @@
         )
 
     def advance(step, carry):
-        a = jnp.sum(jnp.where(flat == my_cell_ref[0], vector_ref[...], 0.0))
+        a = jnp.sum(jnp.where(flat == my_cell, vector_ref[...], 0.0))
         acc = advance_group(step, 0, a)
         for group in range(1, groups):
             acc = acc + advance_group(step, group, a)
@@ -303,7 +310,7 @@
             out_copy(group, distance, beside_me(distance)).wait_recv()
 
 
-def propagate(limit, my_cell, owners, packed, side, weights, stencil, mix, now, old, norm, macro, grid, devices):
+def propagate(materials, kinds, owners, packed, side, weights, stencil, mix, now, old, norm, macro, share, grid, devices):
     groups, _, mine, rows, cells = packed.shape
     planes = grid * mine
     assert planes % BLOCK == 0
@@ -311,7 +318,7 @@
     smem = pl.BlockSpec(memory_space=pltpu.SMEM)
     anywhere = pl.BlockSpec(memory_space=pl.ANY)
     return pl.pallas_call(
-        functools.partial(kernel, norm, macro, grid, devices),
+        functools.partial(kernel, norm, macro, share, grid, devices),
         out_shape=(
             jax.ShapeDtypeStruct(packed.shape, F32),
             jax.ShapeDtypeStruct(now.shape, F32),
@@ -344,7 +351,7 @@
             vmem_limit_bytes=48 * 1024 * 1024, collective_id=0, has_side_effects=True
         ),
         name="propagate",
-    )(limit.reshape(1), my_cell.reshape(1), owners, packed, side, weights, stencil, mix, now, old)
+    )(materials, kinds, owners, packed, side, weights, stencil, mix, now, old)
 
 
 def local(
@@ -356,12 +363,8 @@
     share = grid // points
     own = orb // share
     nproj = projectors.shape[1]
-    micro_index, grid_index = lax.axis_index("micro"), lax.axis_index("grid")
-    first_point = micro_index * points
-    me = first_point + grid_index // share
-    first_orbital = (grid_index % share) * own
+    first_point = lax.axis_index("micro") * points
     kinds = lax.dynamic_slice_in_dim(proj_kind, first_point, points)
-    pick = lambda array: lax.dynamic_index_in_dim(array, me, 0, keepdims=False)
     repeat = lambda array: jnp.repeat(array, share, axis=0)
     packed = (
         orbitals.reshape(2, points, share, GROUPS, own // GROUPS, mine, cells)
@@ -377,23 +380,18 @@
             axis=2,
         )
     )
-    my_weights = strengths[pick(proj_kind)] * (-2.0 * SPACING**2)
-    weights = jnp.broadcast_to(
-        jnp.concatenate([my_weights] * 3 + [jnp.zeros_like(my_weights)])[None], (8, 4 * nproj)
-    )
+    scaled = strengths * (-2.0 * SPACING**2)
+    weights = jnp.concatenate([scaled] * 3 + [jnp.zeros_like(scaled)], axis=1)
     i = lax.broadcasted_iota(jnp.int32, (4 * nproj, 4 * nproj), 0)
     j = lax.broadcasted_iota(jnp.int32, (4 * nproj, 4 * nproj), 1)
     mix = ((i < 2 * nproj) & (i % nproj == j % nproj)).astype(F32)
     stencil = stencil_matrix(cells)
-    my_material = pick(material)
-    my_cell = pick(point_cell)
-    limit = jnp.where(my_material == 1, orb, orb // 2) - first_orbital
     macro = vector_now.shape[0]
     wide = (macro // 1024 + 1) * 1024
     lay = lambda vector: jnp.pad(vector, (0, wide - macro)).reshape(-1, 128)
     field, vector = propagate(
-        limit, my_cell, repeat(point_cell), packed, side, weights, stencil, mix, lay(vector_now), lay(vector_old),
-        2.0 / (orb * grid * mine * cells), macro, grid, devices,
+        repeat(material), repeat(proj_kind), repeat(point_cell), packed, side, weights, stencil, mix, lay(vector_now), lay(vector_old),
+        2.0 / (orb * grid * mine * cells), macro, share, grid, devices,
     )
     field = field.reshape(GROUPS, points, share, mine, 2, own // GROUPS, cells).transpose(4, 1, 2, 0, 5, 3, 6)
     field = field.reshape(2, points, orb, mine, cells)

time: 118 us -> 111 us (0.941)
  local copies, waits for them, and re-layouts: 11.6 us -> 7.99 us
  between operations: 3.38 us -> 0.77 us
    dynamic_slice x3 -> x0, local copies, waits for them, and re-layouts: 3.75 us -> none  [local(): pick = lambda array: lax.dynamic_index_in_dim(array, me, 0, keepdims=False)]
where the time goes in v3:
time: 111 us
  Pallas kernels  101 us (91%)
  local copies, waits for them, and re-layouts  7.99 us (7%)
  other arithmetic  1.2 us (1%)
    pallas_call x1, Pallas kernels, propagate(): pl.pallas_call(functools.partial(kernel, norm, macro, share, grid, device...  101 us
    reshape x1, local copies, waits for them, and re-layouts, local(): field.reshape(GROUPS, points, share, mine, 2, own // GROUPS, cells)  2.96 us

profile of v3, /device:TPU:0, one launch (start us, length us, event | category | flops | bytes accessed | tf_op | source)
XLA Modules:
  0.0 110.8 jit_solution(16383856186968165052)
XLA Ops:
  0.6 0.0 copy-start
  0.6 0.8 dynamic_slice.3
  1.4 0.1 pad.16.clone
  1.5 0.7 broadcast_multiply_fusion
  2.2 0.1 maximum_maximum_fusion.weight_ref
  2.3 0.7 pad_bitcast_fusion
  3.0 0.1 fusion.13.mix_ref
  3.2 0.7 broadcast_in_dim.14
  3.9 0.2 fusion.7
  4.1 0.0 copy-start.4
  4.2 0.0 copy-done
  4.2 1.1 gather_fusion
  5.3 0.1 copy.19
  5.3 0.1 pad_maximum_fusion.packed_side_ref
  5.4 0.3 copy-done.4
  5.7 0.0 copy-start.1
  5.7 0.0 copy-start.2
  5.7 0.3 copy.13
  6.0 0.4 copy-done.1
  6.4 0.0 copy-done.2
  6.4 0.0 copy-done.3
  6.4 100.8 %propagate.1 = (f32[1,8,2,128,256]{4,3,2,1,0:T(8,128)S(1)}, f32[16,128]{1,0:T(8,128)S(1)}) custom-call(s32[32]{0:T(128)S(1)} %copy-done.1, s32[32]{0:T(128)S(1)} %copy-done.2, s32[32]{0:T(128)S(1)} %copy-done.3, f32[1,8,2,128,256]{4,3,2,1,0:T(8,128)S(1)} %bitcast.19, f32[8,2,40,256]{3,2,1,0:T(8,128)S(1)} %pad_maximum_fusion.packed_side_ref, ...), custom_call_target="tpu_custom_call" | custom-call | tf_op jit(solution)/shard_map/propagate/pallas_call | solution.py:320
  107.2 3.0 %copy.18 = f32[1,8,1,2,2,64,256]{6,3,5,1,4,0,2:T(2,128)} copy(f32[1,8,1,2,2,64,256]{6,5,4,3,1,2,0:T(8,128)S(1)} %bitcast.20) | data formatting | bytes 4194304 | tf_op jit(solution)/shard_map/reshape | solution.py:396
  110.2 0.6 copy.21
  (12 shorter events, 0.1 us)
Async XLA Ops:
  0.6 3.5 %copy-start = (f32[2,32,2,256]{3,2,1,0:T(2,128)S(1)}, f32[2,32,2,256]{3,2,1,0:T(2,128)}, u32[]{:S(2)}) copy-start(f32[2,32,2,256]{3,2,1,0:T(2,128)} %param.11) | copy-start | bytes 393220
  4.1 1.6 %copy-start.4 = (f32[2,8,64,2,256]{4,3,2,1,0:T(2,128)S(1)}, f32[2,8,64,2,256]{4,3,2,1,0:T(2,128)}, u32[]{:S(2)}) copy-start(f32[2,8,64,2,256]{4,3,2,1,0:T(2,128)} %param.9) | copy-start | bytes 6291460
  5.7 0.7 copy-start.1
  5.7 0.7 copy-start.2
  5.7 0.7 copy-start.3
